TPU v7x, 512 devices: a whole 4x4x16 slice. The times are simulated.
512 devices in a mesh: ep: 64 (over x_lo, z, core), blk: 8 (over x_hi, y).
Axes of the slice: x: 4 (x_hi: 2, x_lo: 2; x = x_hi * 2 + x_lo), y: 4, z: 16, core: 2. Of those that a mesh axis runs over, the one named last changes fastest.
Arguments:
- tokens: bfloat16 [4096, 2048], P(('ep', 'blk')), may hold values from -6 to 6
- routes: int32 [4096, 8], P('ep'), may hold values from 0 to 63, all different within a row; in each aligned block of 64 rows (0 to 63, 64 to 127, ...) at most 16 rows name the same one
- gate_scale: bfloat16 [4096, 8], P('ep'), may hold values from 0.099609375 to 1
- placement: int32 [64], replicated, may hold values from 0 to 63, each once
- w_gate: bfloat16 [64, 2048, 1024], P('ep', None, 'blk'), may hold values from -0.125 to 0.125
- w_up: bfloat16 [64, 2048, 1024], P('ep', None, 'blk'), may hold values from -0.125 to 0.125
- w_down: bfloat16 [64, 1024, 2048], P('ep', 'blk'), may hold values from -0.1875 to 0.1875
Outputs:
- mixed: bfloat16 [4096, 2048], P(('ep', 'blk'))
Inputs may be any that keep to these rules, and one draw needn't show every extreme that they name: `routes`: in each aligned block of 64 rows (the tokens of one index of ep) no expert is named by more than 16 rows, a bound that some block reaches; a row names 8 different experts. `placement`: each ep index holds exactly one expert.
All inputs are finite; a program needn't handle non-finite values.
Results may differ from a plain program's by a relative error of at most 0.019.
Values may be sent and summed in bfloat16 or wider, within the bound.
A program may use at most 64 MiB of HBM per device.

v0:
```python
import jax
import jax.numpy as jnp
from jax import lax
from jax.sharding import Mesh, PartitionSpec as P

AXES = ("xl", "z", "core", "xh", "y")
EP = ("xl", "z", "core")
BLK = ("xh", "y")
PLANE = ("y", "xh", "xl", "z")


def local(tokens, routes, gate_scale, placement, w_gate, w_up, w_down):
    own = tokens.shape[0]
    experts = placement.shape[0]
    blk_index = lax.axis_index("xh") * lax.axis_size("y") + lax.axis_index("y")
    my_routes = lax.dynamic_slice_in_dim(routes, blk_index * own, own, 0)
    my_scale = lax.dynamic_slice_in_dim(gate_scale, blk_index * own, own, 0)
    ids = lax.iota(jnp.int32, experts)
    chosen = my_routes[:, :, None] == ids[None, None, :]
    holder = jnp.sum(jnp.where(chosen, placement[None, None, :], 0), axis=-1)
    dense = jnp.sum(
        jnp.where(
            holder[:, :, None] == ids[None, None, :], my_scale[:, :, None].astype(jnp.float32), 0.0
        ),
        axis=1,
    ).astype(jnp.bfloat16)
    packed = jnp.concatenate([tokens, dense, jnp.zeros_like(dense)], axis=1)
    everyone = lax.all_gather(packed, "z", axis=0, tiled=True)
    everyone = lax.all_gather(everyone, ("xh", "xl"), axis=0, tiled=True)
    everyone = lax.all_gather(everyone, "y", axis=0, tiled=True)
    width = tokens.shape[1]
    x = everyone[:, :width]
    weights = everyone[:, width : width + experts]
    swap = [(0, 1), (1, 0)]
    wg = jnp.concatenate([w_gate[0], lax.ppermute(w_gate[0], "core", swap)], axis=1)
    wu = jnp.concatenate([w_up[0], lax.ppermute(w_up[0], "core", swap)], axis=1)
    wd = jnp.concatenate([w_down[0], lax.ppermute(w_down[0], "core", swap)], axis=0)
    core = lax.axis_index("core")
    pair = (lax.axis_index("xl") * lax.axis_size("z") + lax.axis_index("z")) * 2
    mine = lax.dynamic_slice_in_dim(weights, pair + core, 1, 1).astype(jnp.float32)
    other = lax.dynamic_slice_in_dim(weights, pair + 1 - core, 1, 1).astype(jnp.float32)
    half = w_down.shape[1]
    first = lax.broadcasted_iota(jnp.int32, (1, 2 * half), 1) < half
    scale = jnp.where(first, mine, other)
    gate = jnp.dot(x, wg, preferred_element_type=jnp.float32)
    up = jnp.dot(x, wu, preferred_element_type=jnp.float32)
    hidden = (jax.nn.silu(gate) * up * scale).astype(jnp.bfloat16)
    out = jnp.dot(hidden, wd, preferred_element_type=jnp.float32).astype(jnp.bfloat16)
    part = lax.psum_scatter(out, "y", scatter_dimension=0, tiled=True)
    part = lax.optimization_barrier(
        lax.psum_scatter(part, ("xh", "xl"), scatter_dimension=0, tiled=True).astype(jnp.float32)
    )
    total = lax.psum_scatter(part, "z", scatter_dimension=0, tiled=True)
    return lax.optimization_barrier(total).astype(jnp.bfloat16)


def solution(mesh):
    fine = Mesh(mesh.devices.reshape(2, 16, 2, 2, 4), AXES)
    in_specs = (
        P(AXES, None),
        P(EP, None),
        P(EP, None),
        P(),
        P(EP, None, BLK),
        P(EP, None, BLK),
        P(EP, BLK, None),
    )
    return jax.shard_map(
        local, mesh=fine, in_specs=in_specs, out_specs=P(AXES, None), check_vma=False
    )
```

profile of v0, /device:TPU:6, one launch (start us, length us, event | category | flops | bytes accessed | tf_op | source)
XLA Modules:
  0.0 417.5 jit_solution(12385986493303225261)
XLA Ops:
  6.6 0.6 copy-done
  7.2 0.1 constant_dynamic-slice_fusion
  7.3 0.1 copy.12
  7.4 0.8 dynamic-slice_convert_fusion
  8.1 0.1 copy.13
  8.2 0.9 select_reduce_fusion.1
  9.1 0.1 select_reduce_fusion
  9.2 0.8 concatenate.12
  10.1 40.7 %all_gather.9 = bf16[128,2176]{1,0:T(8,128)(2,1)} all-gather(bf16[8,2176]{1,0:T(8,128)(2,1)S(1)} %concatenate.12), channel_id=1, replica_groups=mesh['xl'=2,'z'=16,'core'=2,'xh'=2,'y'=4] {'z'}, dimensions={0}, use_global_device_ids=true | all-gather | bytes 591872 | tf_op jit(solution)/shard_map/all_gather | solution.py:28
  50.8 34.0 %all-gather.3.cloned.1.call-done = bf16[512,2176]{1,0:T(8,128)(2,1)} async-done(((bf16[128,2176]{1,0:T(8,128)(2,1)}), bf16[512,2176]{1,0:T(8,128)(2,1)}) %all-gather.3.cloned.1.call-update) | async-done | bytes 2228240 | tf_op jit(solution)/shard_map/all_gather | solution.py:29
  84.9 1.9 collective-permute-start.1
  86.9 2.4 collective-permute-start
  89.3 1.9 collective-permute-start.2
  91.3 92.9 %all-gather.5.cloned.1.call-done = bf16[2048,2176]{1,0:T(8,128)(2,1)} async-done(((bf16[512,2176]{1,0:T(8,128)(2,1)}), bf16[2048,2176]{1,0:T(8,128)(2,1)}) %all-gather.5.cloned.1.call-update) | async-done | bytes 8912912 | tf_op jit(solution)/shard_map/all_gather | solution.py:30
  184.1 1.1 slice.9
  185.2 0.7 convert_reduce_fusion.1
  186.0 7.1 %fusion = f32[2048,256]{1,0:T(8,128)} fusion(bf16[2048,2176]{1,0:T(8,128)(2,1)} %all-gather.5.cloned.1.call-done, bf16[2048,128]{1,0:T(8,128)(2,1)S(1)} %collective-permute-done.1, bf16[2048,128]{1,0:T(8,128)(2,1)S(1)} %bitcast.4), kind=kOutput, calls=%fused_computation.1 | convolution fusion | flops 2149580800 | bytes 11534336 | tf_op jit(solution)/shard_map/dot_general | solution.py:46
  193.1 13.3 %convolution_convert_fusion = bf16[2048,2048]{1,0:T(8,128)(2,1)} fusion(f32[2048,256]{1,0:T(8,128)} %fusion, bf16[128,2048]{1,0:T(8,128)(2,1)S(1)} %collective-permute-done.2, bf16[128,2048]{1,0:T(8,128)(2,1)S(1)} %bitcast.6, f32[2048]{0:T(1024)S(1)} %get-tuple-element.6, f32[2048]{0:T(1024)S(1)} %get-tuple-element.5, ...), kind=kOutput, calls=%fused_computation | convolution fusion | flops 4307550208 | bytes 20988160 | tf_op jit(solution)/shard_map/dot_general | solution.py:48
  206.3 0.0 reduce-scatter.6.cloned.1.call-start
  206.4 89.4 %reduce-scatter.4.cloned.1.call-done = bf16[512,2048]{1,0:T(8,128)(2,1)} async-done(((bf16[2048,2048]{1,0:T(8,128)(2,1)}), bf16[512,2048]{1,0:T(8,128)(2,1)}) %reduce-scatter.4.cloned.1.call-update) | async-done | bytes 2097168 | tf_op jit(solution)/shard_map/reduce_scatter | solution.py:49
  295.9 37.9 %reduce-scatter.6.cloned.1.call-done = bf16[128,2048]{1,0:T(8,128)(2,1)} async-done(((bf16[512,2048]{1,0:T(8,128)(2,1)}), bf16[128,2048]{1,0:T(8,128)(2,1)}) %reduce-scatter.6.cloned.1.call-update) | async-done | bytes 524304 | tf_op jit(solution)/shard_map/reduce_scatter | solution.py:51
  333.8 2.1 convert_element_type.25
  335.9 73.6 %reduce-scatter.8.cloned.1.call-done = f32[8,2048]{1,0:T(8,128)} async-done(((f32[128,2048]{1,0:T(8,128)}), f32[8,2048]{1,0:T(8,128)}) %reduce-scatter.8.cloned.1.call-update) | async-done | bytes 65552 | tf_op jit(solution)/shard_map/reduce_scatter | solution.py:53
  409.5 1.5 convert_element_type.26
  (21 shorter events, 0.3 us)
Async XLA Ops:
  6.5 0.7 copy-start
  6.5 78.4 %copy-start.1 = (bf16[1,2048,128]{2,1,0:T(8,128)(2,1)S(1)}, bf16[1,2048,128]{2,1,0:T(8,128)(2,1)}, u32[]{:S(2)}) copy-start(bf16[1,2048,128]{2,1,0:T(8,128)(2,1)} %param.12) | copy-start | bytes 1572868
  6.5 80.3 %copy-start.3 = (bf16[1,2048,128]{2,1,0:T(8,128)(2,1)S(1)}, bf16[1,2048,128]{2,1,0:T(8,128)(2,1)}, u32[]{:S(2)}) copy-start(bf16[1,2048,128]{2,1,0:T(8,128)(2,1)} %param.11) | copy-start | bytes 1572868
  6.5 82.7 %copy-start.2 = (bf16[1,128,2048]{2,1,0:T(8,128)(2,1)S(1)}, bf16[1,128,2048]{2,1,0:T(8,128)(2,1)}, u32[]{:S(2)}) copy-start(bf16[1,128,2048]{2,1,0:T(8,128)(2,1)} %param.13) | copy-start | bytes 1572868
  6.5 78.3 %all-gather.3.cloned.1.call-start = ((), (), s32[]{:S(2)}) async-start(), calls=%async_computation.3 | async-start | bytes 2785280 | tf_op jit(solution)/shard_map/all_gather | solution.py:29
  50.8 133.3 %all-gather.5.cloned.1.call-start = ((), (), s32[]{:S(2)}) async-start(), calls=%async_computation.4 | async-start | bytes 11141120 | tf_op jit(solution)/shard_map/all_gather | solution.py:30
  84.9 210.9 %reduce-scatter.4.cloned.1.call-start = ((), (), s32[]{:S(2)}) async-start(), calls=%async_computation.5 | async-start | bytes 10485760 | tf_op jit(solution)/shard_map/reduce_scatter | solution.py:49
  84.9 101.0 %collective-permute-start.1 = (bf16[2048,128]{1,0:T(8,128)(2,1)S(1)}, bf16[2048,128]{1,0:T(8,128)(2,1)S(1)}, u32[]{:S(2)}, u32[]{:S(2)}) collective-permute-start(bf16[2048,128]{1,0:T(8,128)(2,1)S(1)} %bitcast.3), channel_id=1, source_target_pairs={{0,8},{8,0},{1,9},{9,1},{2,10},{10,2},{3,11},{11,3},{4,12},{12,4},... | collective-permute-start | bytes 1572872 | tf_op jit(solution)/shard_map/ppermute | solution.py:36
  86.9 106.2 %collective-permute-start = (bf16[2048,128]{1,0:T(8,128)(2,1)S(1)}, bf16[2048,128]{1,0:T(8,128)(2,1)S(1)}, u32[]{:S(2)}, u32[]{:S(2)}) collective-permute-start(bf16[2048,128]{1,0:T(8,128)(2,1)S(1)} %bitcast.7), channel_id=1, source_target_pairs={{0,8},{8,0},{1,9},{9,1},{2,10},{10,2},{3,11},{11,3},{4,12},{12,4},... | collective-permute-start | bytes 1572872 | tf_op jit(solution)/shard_map/ppermute | solution.py:35
  89.3 103.8 %collective-permute-start.2 = (bf16[128,2048]{1,0:T(8,128)(2,1)S(1)}, bf16[128,2048]{1,0:T(8,128)(2,1)S(1)}, u32[]{:S(2)}, u32[]{:S(2)}) collective-permute-start(bf16[128,2048]{1,0:T(8,128)(2,1)S(1)} %bitcast.5), channel_id=1, source_target_pairs={{0,8},{8,0},{1,9},{9,1},{2,10},{10,2},{3,11},{11,3},{4,12},{12,4},... | collective-permute-start | bytes 1572872 | tf_op jit(solution)/shard_map/ppermute | solution.py:37
  206.3 127.5 %reduce-scatter.6.cloned.1.call-start = ((), (), s32[]{:S(2)}) async-start(), calls=%async_computation.6 | async-start | bytes 2621440 | tf_op jit(solution)/shard_map/reduce_scatter | solution.py:51
  295.8 113.7 %reduce-scatter.8.cloned.1.call-start = ((), (), s32[]{:S(2)}) async-start(), calls=%async_computation.7 | async-start | bytes 1114112 | tf_op jit(solution)/shard_map/reduce_scatter | solution.py:53
Sparse Core Ops, SparseCore 0:
  50.9 33.8 all-gather.2
  86.9 97.1 all-gather.4
  206.5 89.2 reduce-scatter.3
  298.5 35.2 reduce-scatter.5
  336.5 73.0 reduce-scatter.7
where the time goes:
time: 418 us
  waiting for transfers between devices  328 us (78%)
  blocking collectives  40.7 us (10%)
  matrix products  20.4 us (5%)
  between operations  13.3 us (3%)
  starting transfers between devices  6.44 us (2%)
  other arithmetic  6.1 us (1%)
    all_gather x1, waiting for transfers between devices, local(): everyone = lax.all_gather(everyone, 'y', axis=0, tiled=True)  92.9 us
    reduce_scatter x1, waiting for transfers between devices, local(): part = lax.psum_scatter(out, 'y', scatter_dimension=0, tiled=True)  89.4 us
    reduce_scatter x1, waiting for transfers between devices, local(): total = lax.psum_scatter(part, 'z', scatter_dimension=0, tiled=True)  73.6 us
    all_gather x1, blocking collectives, local(): everyone = lax.all_gather(packed, 'z', axis=0, tiled=True)  40.7 us
    reduce_scatter x1, waiting for transfers between devices, local(): lax.psum_scatter(part, ('xh', 'xl'), scatter_dimension=0, tiled=True)  37.9 us
    all_gather x1, waiting for transfers between devices, local(): everyone = lax.all_gather(everyone, ('xh', 'xl'), axis=0, tiled=True)  34 us
    dot_general x1, matrix products, local(): jnp.dot(hidden, wd, preferred_element_type=jnp.float32).astype(jnp.bfloat16)  13.3 us
  transfers between devices with their start and end apart: 8, of which 5 were waited for; matrix products, arithmetic and copies ran while one was open for 2% of the time, Pallas kernels for 0%

commit v1 on v0

--- a/solution.py
+++ b/solution.py
@@ -26,7 +26,10 @@
     ).astype(jnp.bfloat16)
     packed = jnp.concatenate([tokens, dense, jnp.zeros_like(dense)], axis=1)
     everyone = lax.all_gather(packed, "z", axis=0, tiled=True)
-    everyone = lax.all_gather(everyone, ("xh", "xl"), axis=0, tiled=True)
+    everyone = jnp.concatenate(
+        lax.all_to_all(jnp.stack([everyone] * lax.axis_size(("xh", "xl"))), ("xh", "xl"), 0, 0),
+        axis=0,
+    )
     everyone = lax.all_gather(everyone, "y", axis=0, tiled=True)
     width = tokens.shape[1]
     x = everyone[:, :width]

time: 418 us -> 400 us (0.957)
  waiting for transfers between devices: 328 us -> 285 us
  blocking collectives: 40.7 us -> 61.4 us
  local copies, waits for them, and re-layouts: 2.78 us -> 7.15 us
    all_gather x1 -> x0, waiting for transfers between devices: 34 us -> none  [local(): everyone = lax.all_gather(everyone, ('xh', 'xl'), axis=0, tiled=True)]
    all_to_all x0 -> x1, blocking collectives: none -> 22.7 us  [local(): lax.all_to_all(jnp.stack([everyone] * lax.axis_size(('xh', 'xl'))), ('xh'...]
    all_gather x1, waiting for transfers between devices: 92.9 us -> 84.2 us  [local(): everyone = lax.all_gather(everyone, 'y', axis=0, tiled=True)]
  transfers between devices with their start and end apart: 8 -> 7, of which waited for: 5 -> 4; matrix products, arithmetic and copies ran while one was open for 2% -> 2% of each run, Pallas kernels for 0% -> 0%
where the time goes in v1:
time: 400 us
  waiting for transfers between devices  285 us (71%)
  blocking collectives  61.4 us (15%)
  matrix products  20.4 us (5%)
  between operations  13.2 us (3%)
  local copies, waits for them, and re-layouts  7.15 us (2%)
  starting transfers between devices  6.36 us (2%)
  other arithmetic  6.12 us (2%)
    reduce_scatter x1, waiting for transfers between devices, local(): part = lax.psum_scatter(out, 'y', scatter_dimension=0, tiled=True)  89.4 us
    all_gather x1, waiting for transfers between devices, local(): everyone = lax.all_gather(everyone, 'y', axis=0, tiled=True)  84.2 us
    reduce_scatter x1, waiting for transfers between devices, local(): total = lax.psum_scatter(part, 'z', scatter_dimension=0, tiled=True)  73.6 us
    all_gather x1, blocking collectives, local(): everyone = lax.all_gather(packed, 'z', axis=0, tiled=True)  38.7 us
    reduce_scatter x1, waiting for transfers between devices, local(): lax.psum_scatter(part, ('xh', 'xl'), scatter_dimension=0, tiled=True)  38.1 us
    all_to_all x1, blocking collectives, local(): lax.all_to_all(jnp.stack([everyone] * lax.axis_size(('xh', 'xl'))), ('xh'...  22.7 us
    dot_general x1, matrix products, local(): jnp.dot(hidden, wd, preferred_element_type=jnp.float32).astype(jnp.bfloat16)  13.3 us
  transfers between devices with their start and end apart: 7, of which 4 were waited for; matrix products, arithmetic and copies ran while one was open for 2% of the time, Pallas kernels for 0%

profile of v1, /device:TPU:6, one launch (start us, length us, event | category | flops | bytes accessed | tf_op | source)
XLA Modules:
  0.0 399.9 jit_solution(3073677802018992655)
XLA Ops:
  6.5 0.7 copy-done
  7.4 0.8 dynamic-slice_convert_fusion
  8.2 0.9 select_reduce_fusion.1
  9.1 0.1 select_reduce_fusion
  9.2 0.8 concatenate.12
  10.1 38.7 %all_gather.6 = bf16[128,2176]{1,0:T(8,128)(2,1)S(1)} all-gather(bf16[8,2176]{1,0:T(8,128)(2,1)S(1)} %concatenate.12), channel_id=1, replica_groups=mesh['xl'=2,'z'=16,'core'=2,'xh'=2,'y'=4] {'z'}, dimensions={0}, use_global_device_ids=true | all-gather | bytes 591872 | tf_op jit(solution)/shard_map/all_gather | solution.py:28
  48.8 0.3 copy.22
  49.1 0.3 stack.2
  49.4 22.7 %all_to_all.5 = bf16[4,128,2176]{1,2,0:T(8,128)(2,1)S(1)} all-to-all(bf16[4,128,2176]{1,2,0:T(8,128)(2,1)S(1)} %stack.2), channel_id=1, replica_groups=mesh['xl'=2,'z'=16,'core'=2,'xh'=2,'y'=4] {'xh','xl'}, dimensions={0} | all-to-all | bytes 4456448 | tf_op jit(solution)/shard_map/all_to_all | solution.py:30
  72.1 2.7 copy.23
  74.9 1.0 copy-done.1
  75.9 1.9 collective-permute-start.1
  77.8 2.4 collective-permute-start
  80.2 1.9 collective-permute-start.2
  82.2 84.2 %all-gather.2.cloned.1.call-done = bf16[2048,2176]{1,0:T(8,128)(2,1)} async-done(((bf16[512,2176]{1,0:T(8,128)(2,1)}), bf16[2048,2176]{1,0:T(8,128)(2,1)}) %all-gather.2.cloned.1.call-update) | async-done | bytes 8912912 | tf_op jit(solution)/shard_map/all_gather | solution.py:33
  166.4 1.1 slice.9
  167.5 0.7 convert_reduce_fusion.1
  168.2 7.1 %fusion = f32[2048,256]{1,0:T(8,128)} fusion(bf16[2048,2176]{1,0:T(8,128)(2,1)} %all-gather.2.cloned.1.call-done, bf16[2048,128]{1,0:T(8,128)(2,1)S(1)} %collective-permute-done.1, bf16[2048,128]{1,0:T(8,128)(2,1)S(1)} %bitcast.6), kind=kOutput, calls=%fused_computation.1 | convolution fusion | flops 2149580800 | bytes 11534336 | tf_op jit(solution)/shard_map/dot_general | solution.py:49
  175.3 13.3 %convolution_convert_fusion = bf16[2048,2048]{1,0:T(8,128)(2,1)} fusion(f32[2048,256]{1,0:T(8,128)} %fusion, bf16[128,2048]{1,0:T(8,128)(2,1)S(1)} %collective-permute-done.2, bf16[128,2048]{1,0:T(8,128)(2,1)S(1)} %bitcast.8, f32[2048]{0:T(1024)S(1)} %get-tuple-element.6, f32[2048]{0:T(1024)S(1)} %get-tuple-element.5, ...), kind=kOutput, calls=%fused_computation | convolution fusion | flops 4307550208 | bytes 20988160 | tf_op jit(solution)/shard_map/dot_general | solution.py:51
  188.7 89.4 %reduce-scatter.4.cloned.1.call-done = bf16[512,2048]{1,0:T(8,128)(2,1)} async-done(((bf16[2048,2048]{1,0:T(8,128)(2,1)}), bf16[512,2048]{1,0:T(8,128)(2,1)}) %reduce-scatter.4.cloned.1.call-update) | async-done | bytes 2097168 | tf_op jit(solution)/shard_map/reduce_scatter | solution.py:52
  278.1 38.1 %reduce-scatter.6.cloned.1.call-done = bf16[128,2048]{1,0:T(8,128)(2,1)} async-done(((bf16[512,2048]{1,0:T(8,128)(2,1)}), bf16[128,2048]{1,0:T(8,128)(2,1)}) %reduce-scatter.6.cloned.1.call-update) | async-done | bytes 524304 | tf_op jit(solution)/shard_map/reduce_scatter | solution.py:54
  316.2 2.1 convert_element_type.25
  318.4 73.6 %reduce-scatter.8.cloned.1.call-done = f32[8,2048]{1,0:T(8,128)} async-done(((f32[128,2048]{1,0:T(8,128)}), f32[8,2048]{1,0:T(8,128)}) %reduce-scatter.8.cloned.1.call-update) | async-done | bytes 65552 | tf_op jit(solution)/shard_map/reduce_scatter | solution.py:56
  392.0 1.5 convert_element_type.26
  (22 shorter events, 0.4 us)
Async XLA Ops:
  6.5 0.7 copy-start
  6.5 159.9 %all-gather.2.cloned.1.call-start = ((), (), s32[]{:S(2)}) async-start(), calls=%async_computation.4 | async-start | bytes 11141120 | tf_op jit(solution)/shard_map/all_gather | solution.py:33
  74.8 1.0 copy-start.1
  74.8 3.0 copy-start.3
  74.8 5.4 %copy-start.2 = (bf16[1,128,2048]{2,1,0:T(8,128)(2,1)S(1)}, bf16[1,128,2048]{2,1,0:T(8,128)(2,1)}, u32[]{:S(2)}) copy-start(bf16[1,128,2048]{2,1,0:T(8,128)(2,1)} %param.13) | copy-start | bytes 1572868
  74.8 203.2 %reduce-scatter.4.cloned.1.call-start = ((), (), s32[]{:S(2)}) async-start(), calls=%async_computation.5 | async-start | bytes 10485760 | tf_op jit(solution)/shard_map/reduce_scatter | solution.py:52
  75.9 92.4 %collective-permute-start.1 = (bf16[2048,128]{1,0:T(8,128)(2,1)S(1)}, bf16[2048,128]{1,0:T(8,128)(2,1)S(1)}, u32[]{:S(2)}, u32[]{:S(2)}) collective-permute-start(bf16[2048,128]{1,0:T(8,128)(2,1)S(1)} %bitcast.5), channel_id=1, source_target_pairs={{0,8},{8,0},{1,9},{9,1},{2,10},{10,2},{3,11},{11,3},{4,12},{12,4},... | collective-permute-start | bytes 1572872 | tf_op jit(solution)/shard_map/ppermute | solution.py:39
  77.8 97.5 %collective-permute-start = (bf16[2048,128]{1,0:T(8,128)(2,1)S(1)}, bf16[2048,128]{1,0:T(8,128)(2,1)S(1)}, u32[]{:S(2)}, u32[]{:S(2)}) collective-permute-start(bf16[2048,128]{1,0:T(8,128)(2,1)S(1)} %bitcast.9), channel_id=1, source_target_pairs={{0,8},{8,0},{1,9},{9,1},{2,10},{10,2},{3,11},{11,3},{4,12},{12,4},... | collective-permute-start | bytes 1572872 | tf_op jit(solution)/shard_map/ppermute | solution.py:38
  80.2 95.1 %collective-permute-start.2 = (bf16[128,2048]{1,0:T(8,128)(2,1)S(1)}, bf16[128,2048]{1,0:T(8,128)(2,1)S(1)}, u32[]{:S(2)}, u32[]{:S(2)}) collective-permute-start(bf16[128,2048]{1,0:T(8,128)(2,1)S(1)} %bitcast.7), channel_id=1, source_target_pairs={{0,8},{8,0},{1,9},{9,1},{2,10},{10,2},{3,11},{11,3},{4,12},{12,4},... | collective-permute-start | bytes 1572872 | tf_op jit(solution)/shard_map/ppermute | solution.py:40
  188.6 127.6 %reduce-scatter.6.cloned.1.call-start = ((), (), s32[]{:S(2)}) async-start(), calls=%async_computation.6 | async-start | bytes 2621440 | tf_op jit(solution)/shard_map/reduce_scatter | solution.py:54
  278.1 113.9 %reduce-scatter.8.cloned.1.call-start = ((), (), s32[]{:S(2)}) async-start(), calls=%async_computation.7 | async-start | bytes 1114112 | tf_op jit(solution)/shard_map/reduce_scatter | solution.py:56
Sparse Core Ops, SparseCore 0:
  75.0 91.3 all-gather.1
  188.7 89.2 reduce-scatter.3
  280.9 35.2 reduce-scatter.5
  318.9 73.0 reduce-scatter.7
